TPU v7x, 32 devices: a whole 2x2x4 slice. The times are simulated.
32 devices in a mesh: dp: 8 (over z, y), expert: 4 (over x, core).
Axes of the slice: x: 2, y: 2, z: 4, core: 2. Of those that a mesh axis runs over, the one named last changes fastest.
Arguments:
- tokens: bfloat16 [1024, 4096], P('dp'), may hold values from -6 to 6
- upstream: bfloat16 [1024, 4096], P('dp', 'expert'), may hold values from -6 to 6
- gates: bfloat16 [1024, 2], P('dp'), may hold values from 0.049804688 to 1
- expert_ids: int32 [1024, 2], P('dp'), may hold values from 0 to 7, all different within a row; in each aligned block of 128 rows (0 to 127, 128 to 255, ...) at most 64 rows name the same one
- w_gate: bfloat16 [8, 1536, 4096], P('dp', 'expert'), may hold values from -0.09375 to 0.09375
- w_up: bfloat16 [8, 1536, 4096], P('dp', 'expert'), may hold values from -0.09375 to 0.09375
- w_down: bfloat16 [8, 1536, 4096], P('dp', 'expert'), may hold values from -0.15625 to 0.15625
Outputs:
- grad_x: bfloat16 [1024, 4096], P('dp', 'expert')
- grad_gates: float32 [1024, 2], P('dp')
- grad_w_gate: bfloat16 [8, 1536, 4096], P('dp', 'expert')
- grad_w_up: bfloat16 [8, 1536, 4096], P('dp', 'expert')
- grad_w_down: bfloat16 [8, 1536, 4096], P('dp', 'expert')
Inputs may be any that keep to these rules, and one draw needn't show every extreme that they name: `expert_ids`: each row names 2 different experts. In each aligned block of 128 rows (the tokens of one index of dp) no expert is named by more than 64 rows, a bound that some block reaches.
All inputs are finite; a program needn't handle non-finite values.
Results may differ from a plain program's by a relative error of at most 0.012.
Values may be sent and summed in bfloat16 or wider, within the bound.
A program may use at most 128 MiB of HBM per device.

v0:
```python
import jax
import jax.numpy as jnp
from jax import lax
from jax.sharding import PartitionSpec as P


def swish_pair(pre):
    sigma = jax.nn.sigmoid(pre)
    return (pre * sigma, sigma * (1.0 + pre * (1.0 - sigma)))


def contract_last(left, right):
    return lax.dot_general(
        left, right, (((1,), (1,)), ((), ())), preferred_element_type=jnp.float32
    )


def contract_first(left, right):
    return lax.dot_general(
        left, right, (((0,), (0,)), ((), ())), preferred_element_type=jnp.float32
    )


def expert_backward(inputs, upward, scales, w_g, w_u, w_d):
    pre_gate = contract_last(inputs, w_g)
    pre_up = contract_last(inputs, w_u)
    swish, slope = swish_pair(pre_gate)
    act = (swish * pre_up).astype(jnp.bfloat16)
    act_f = act.astype(jnp.float32)
    back = contract_last(upward, w_d)
    gate_term = jnp.sum(act_f * back, axis=1)
    scale_col = scales.astype(jnp.float32)[:, None]
    scaled = (scale_col * act_f).astype(jnp.bfloat16)
    grad_down = contract_first(scaled, upward).astype(jnp.bfloat16)
    weighted = scale_col * back
    d_gate = (weighted * pre_up * slope).astype(jnp.bfloat16)
    d_up = (weighted * swish).astype(jnp.bfloat16)
    grad_gate = contract_first(d_gate, inputs).astype(jnp.bfloat16)
    grad_up = contract_first(d_up, inputs).astype(jnp.bfloat16)
    piece = jnp.dot(d_gate, w_g, preferred_element_type=jnp.float32)
    piece = piece + jnp.dot(d_up, w_u, preferred_element_type=jnp.float32)
    piece = lax.optimization_barrier(piece.astype(jnp.bfloat16))
    return (piece, gate_term, grad_gate, grad_up, grad_down)


def per_device(tokens, upstream, gates, expert_ids, w_gate, w_up, w_down):
    groups = lax.axis_size("dp")
    local = w_gate.shape[0]
    experts = groups * local
    tok_rows = tokens.shape[0]
    width = tokens.shape[1]
    top = expert_ids.shape[1]
    cap = 2 * tok_rows * top // experts
    full_up = lax.all_gather(upstream, "expert", axis=1, tiled=True)
    flat_ids = expert_ids.reshape(-1)
    onehot = (flat_ids[:, None] == jnp.arange(experts, dtype=jnp.int32)[None, :]).astype(jnp.int32)
    position = jnp.sum((jnp.cumsum(onehot, axis=0) - onehot) * onehot, axis=1)
    slot = flat_ids * cap + position
    count = flat_ids.shape[0]
    owner = (
        jnp.zeros((experts * cap,), jnp.int32).at[slot].set(jnp.arange(count, dtype=jnp.int32) + 1)
    )
    live = owner > 0
    source = jnp.maximum(owner - 1, 0)
    token_of = source // top
    send_rows = jnp.where(live[:, None], tokens[token_of], jnp.zeros((), jnp.bfloat16))
    send_up = jnp.where(live[:, None], full_up[token_of], jnp.zeros((), jnp.bfloat16))
    send_scale = jnp.where(live, gates.reshape(-1)[source], jnp.zeros((), jnp.bfloat16))
    got_rows, got_up, got_scale = (
        lax.all_to_all(send_rows, "dp", split_axis=0, concat_axis=0, tiled=True),
        lax.all_to_all(send_up, "dp", split_axis=0, concat_axis=0, tiled=True),
        lax.all_to_all(send_scale, "dp", split_axis=0, concat_axis=0, tiled=True),
    )
    got_rows = got_rows.reshape(groups, local, cap, width)
    got_up = got_up.reshape(groups, local, cap, width)
    got_scale = got_scale.reshape(groups, local, cap)
    pieces, terms, grads_gate, grads_up, grads_down = ([], [], [], [], [])
    result = expert_backward(
        got_rows[:, 0].reshape(groups * cap, width),
        got_up[:, 0].reshape(groups * cap, width),
        got_scale[:, 0].reshape(groups * cap),
        w_gate[0],
        w_up[0],
        w_down[0],
    )
    pieces.append(result[0].reshape(groups, cap, width))
    terms.append(result[1].reshape(groups, cap))
    grads_gate.append(result[2])
    grads_up.append(result[3])
    grads_down.append(result[4])
    part_all = jnp.stack(pieces, axis=1).reshape(groups * local * cap, width)
    term_all = jnp.stack(terms, axis=1).reshape(groups * local * cap)
    gate_total = lax.psum(term_all, "expert")
    summed = lax.psum_scatter(
        part_all.astype(jnp.float32).astype(jnp.bfloat16), "expert", scatter_dimension=1, tiled=True
    ).astype(jnp.float32)
    back_rows, back_terms = (
        lax.all_to_all(summed, "dp", split_axis=0, concat_axis=0, tiled=True),
        lax.all_to_all(gate_total, "dp", split_axis=0, concat_axis=0, tiled=True),
    )
    grad_x = jnp.sum(back_rows[slot].reshape(tok_rows, top, -1), axis=1).astype(jnp.bfloat16)
    grad_gates = back_terms[slot].reshape(tok_rows, top)
    return (grad_x, grad_gates, jnp.stack(grads_gate), jnp.stack(grads_up), jnp.stack(grads_down))


def solution(mesh):
    in_specs = (
        P("dp", None),
        P("dp", "expert"),
        P("dp", None),
        P("dp", None),
        P("dp", "expert", None),
        P("dp", "expert", None),
        P("dp", "expert", None),
    )
    out_specs = (
        P("dp", "expert"),
        P("dp", None),
        P("dp", "expert", None),
        P("dp", "expert", None),
        P("dp", "expert", None),
    )
    return jax.shard_map(
        per_device, mesh=mesh, in_specs=in_specs, out_specs=out_specs, check_vma=False
    )
```

profile of v0, /device:TPU:0, one launch (start us, length us, event | category | flops | bytes accessed | tf_op | source)
XLA Modules:
  0.0 376.8 jit_solution(7693159166872950793)
XLA Ops:
  7.2 0.7 all-gather.2.cloned.1.call-update
  7.9 1.0 copy.18
  8.9 0.1 eq.29
  9.0 0.1 eq.25
  9.2 0.7 broadcast_multiply_fusion
  9.9 0.1 copy.17
  10.0 0.1 mul.59
  10.1 0.6 reduce-window.6
  10.7 0.2 slice_reduce_fusion
  11.0 0.8 copy.20
  11.8 0.1 reshape.96
  11.9 0.1 fusion.18
  12.0 1.4 scatter_custom_fusion
  13.5 3.4 gather_fusion
  16.8 0.7 all_to_all.50
  17.5 7.3 %all-to-all-start = ((bf16[8,64,1]{1,2,0:T(2,128)(2,1)}), bf16[8,64,1]{1,2,0:T(2,128)(2,1)S(1)}, u32[]{:S(2)}, u32[]{:S(2)}) async-start(bf16[8,64,1]{1,2,0:T(2,128)(2,1)} %all_to_all.50), calls=%async_computation | async-start | bytes 8192 | tf_op jit(solution)/shard_map/all_to_all | solution.py:72
  24.8 0.1 broadcast_in_dim.38
  24.9 10.0 %gather_fusion.2 = bf16[512,4096]{1,0:T(8,128)(2,1)} fusion(bf16[128,4096]{1,0:T(8,128)(2,1)} %param.7, s32[1024]{0:T(1024)S(1)} %pad_clamp_fusion.1), kind=kCustom, calls=%fused_computation.2 | custom fusion | bytes 8390656 | tf_op jit(solution)/shard_map/gather | solution.py:66
  34.9 9.9 %gather_fusion.1 = bf16[512,4096]{1,0:T(8,128)(2,1)} fusion(bf16[128,4096]{1,0:T(8,128)(2,1)} %all-gather.2.cloned.1.call-done, s32[1024]{0:T(1024)S(1)} %pad_clamp_fusion.1), kind=kCustom, calls=%fused_computation.1 | custom fusion | bytes 8390656 | tf_op jit(solution)/shard_map/gather | solution.py:67
  44.8 5.8 %broadcast_select_fusion.1 = (bf16[8,64,4096]{2,1,0:T(8,128)(2,1)}, bf16[8,64,4096]{2,1,0:T(8,128)(2,1)}) fusion(bf16[8,64,4096]{2,1,0:T(8,128)(2,1)} %bitcast.51, pred[8,64]{1,0:T(8,128)(4,1)S(1)} %broadcast_in_dim.38, bf16[8,64,4096]{2,1,0:T(8,128)(2,1)} %bitcast.50), kind=kLoop, calls=%fused_computation.14 | loop fusion | flops 4194304 | bytes 16777728 | tf_op jit(solution)/shard_map/jit(_where)/select_n | solution.py:67
  50.6 99.0 %all_to_all.56 = bf16[8,64,4096]{2,1,0:T(8,128)(2,1)} all-to-all(bf16[8,64,4096]{2,1,0:T(8,128)(2,1)} %get-tuple-element.24), channel_id=1, replica_groups=mesh['dp'=8,'expert'=4] {'dp'}, dimensions={0} | all-to-all | bytes 8388608 | tf_op jit(solution)/shard_map/all_to_all | solution.py:70
  149.6 4.5 %all-to-all-start.1 = ((bf16[8,64,4096]{2,1,0:T(8,128)(2,1)}), bf16[8,64,4096]{2,1,0:T(8,128)(2,1)}, u32[]{:S(2)}, u32[]{:S(2)}) async-start(bf16[8,64,4096]{2,1,0:T(8,128)(2,1)} %get-tuple-element.23), calls=%async_computation.1 | async-start | bytes 8388608 | tf_op jit(solution)/shard_map/all_to_all | solution.py:71
  154.1 0.2 reduce-scatter.2.cloned.1.call-start
  154.4 0.1 reshape.99
  154.4 6.0 %fusion.8 = f32[512,384]{0,1:T(8,128)} fusion(bf16[512,4096]{1,0:T(8,128)(2,1)} %bitcast.52, bf16[1,384,4096]{2,1,0:T(8,128)(2,1)} %param.12), kind=kOutput, calls=%fused_computation.20 | convolution fusion | flops 1610612736 | bytes 8126464 | tf_op jit(solution)/shard_map/dot_general | solution.py:13
  160.4 2.8 fusion.5
  163.2 83.1 %all-to-all-done.1 = bf16[8,64,4096]{2,1,0:T(8,128)(2,1)} async-done(((bf16[8,64,4096]{2,1,0:T(8,128)(2,1)}), bf16[8,64,4096]{2,1,0:T(8,128)(2,1)}, u32[]{:S(2)}, u32[]{:S(2)}) %all-to-all-start.1) | async-done | bytes 4194336 | tf_op jit(solution)/shard_map/all_to_all | solution.py:71
  246.3 6.4 %fusion.12 = (f32[512]{0:T(512)S(1)}, bf16[512,384]{0,1:T(8,128)(2,1)}, bf16[512,384]{0,1:T(8,128)(2,1)S(1)}, bf16[512,384]{0,1:T(8,128)(2,1)S(1)}) fusion(f32[512,384]{0,1:T(8,128)} %fusion.8, f32[512,384]{0,1:T(8,128)} %fusion.5, f32[512]{0:T(512)S(1)} %reshape.99, bf16[512,4096]{1,0:T(8,128)(2,1)} %bitcast.5, bf16[1,384,4096]{2,1,0:T(8,128)(2,1)} %param.13), kind=kOutput, calls=%fused_computation.26 | convolution fusion | flops 1614347776 | bytes 10096640 | tf_op jit(solution)/shard_map/dot_general | solution.py:13
  252.7 2.4 fusion.3
  255.1 4.6 %add_convert_fusion = bf16[512,4096]{1,0:T(8,128)(2,1)} fusion(f32[512,4096]{1,0:T(8,128)S(1)} %fusion.3, bf16[512,384]{0,1:T(8,128)(2,1)S(1)} %get-tuple-element.20, bf16[1,384,4096]{2,1,0:T(8,128)(2,1)S(1)} %copy-done.3), kind=kOutput, calls=%fused_computation.6 | convolution fusion | flops 1614807040 | bytes 16121856 | tf_op jit(solution)/shard_map/dot_general | solution.py:41
  259.7 0.1 all_to_all.46
  259.8 6.2 %psum.7 = f32[8,64,1]{1,0,2:T(8,128)} all-reduce(f32[8,64,1]{1,0,2:T(8,128)S(1)} %all_to_all.46), channel_id=1, replica_groups=mesh['dp'=8,'expert'=4] {'expert'}, use_global_device_ids=true, to_apply=%region_7.8 | all-reduce | flops 512 | bytes 4096 | tf_op jit(solution)/shard_map/psum | solution.py:93
  266.0 4.8 %all-to-all-start.4 = ((f32[8,64,1]{1,2,0:T(1,128)}), f32[8,64,1]{1,2,0:T(1,128)S(1)}, u32[]{:S(2)}, u32[]{:S(2)}) async-start(f32[8,64,1]{1,2,0:T(1,128)} %bitcast.13), calls=%async_computation.5 | async-start | bytes 8192 | tf_op jit(solution)/shard_map/all_to_all | solution.py:99
  270.8 32.5 %reduce-scatter.2.cloned.1.call-done = bf16[512,1024]{1,0:T(8,128)(2,1)} async-done(((bf16[512,4096]{1,0:T(8,128)(2,1)}), bf16[512,1024]{1,0:T(8,128)(2,1)}) %reduce-scatter.2.cloned.1.call-update) | async-done | bytes 1048592 | tf_op jit(solution)/shard_map/reduce_scatter | solution.py:94
  303.3 2.8 convert.2
  306.1 5.5 %all-to-all-start.3 = ((f32[8,64,1024]{2,1,0:T(8,128)}), f32[8,64,1024]{2,1,0:T(8,128)}, u32[]{:S(2)}, u32[]{:S(2)}) async-start(f32[8,64,1024]{2,1,0:T(8,128)} %convert.2), calls=%async_computation.4 | async-start | bytes 4194304 | tf_op jit(solution)/shard_map/all_to_all | solution.py:98
  311.6 5.9 %fusion = bf16[1,384,4096]{2,1,0:T(8,128)(2,1)} fusion(bf16[512,384]{0,1:T(8,128)(2,1)} %copy-done.4, bf16[512,4096]{1,0:T(8,128)(2,1)} %bitcast.53), kind=kOutput, calls=%fused_computation.10 | convolution fusion | flops 1612185600 | bytes 7733248 | tf_op jit(solution)/shard_map/dot_general | solution.py:19
  317.5 3.5 fusion.1
  321.1 5.7 %fusion.2 = bf16[1,384,4096]{2,1,0:T(8,128)(2,1)} fusion(bf16[512,4096]{1,0:T(8,128)(2,1)} %bitcast.5, bf16[512,384]{0,1:T(8,128)(2,1)S(1)} %copy-done.5, f32[512]{0:T(512)S(1)} %reshape.99), kind=kOutput, calls=%fused_computation.12 | convolution fusion | flops 1612775424 | bytes 7735296 | tf_op jit(solution)/shard_map/dot_general | solution.py:19
  326.7 0.5 broadcast.122
  327.2 0.7 reduce.9
  328.0 1.9 gather_fusion.4
  329.9 0.1 reshape.98
  330.1 0.6 copy.23
  330.7 29.0 %all-to-all-done.3 = f32[8,64,1024]{2,1,0:T(8,128)} async-done(((f32[8,64,1024]{2,1,0:T(8,128)}), f32[8,64,1024]{2,1,0:T(8,128)}, u32[]{:S(2)}, u32[]{:S(2)}) %all-to-all-start.3) | async-done | bytes 2097184 | tf_op jit(solution)/shard_map/all_to_all | solution.py:98
  359.8 4.1 %gather_fusion.3 = f32[256,1024]{1,0:T(8,128)} fusion(f32[512,1024]{1,0:T(8,128)} %bitcast.12, s32[1024]{0:T(1024)S(1)} %pad_clamp_fusion), kind=kCustom, calls=%fused_computation.3 | custom fusion | bytes 2098176 | tf_op jit(solution)/shard_map/gather | solution.py:101
  363.9 2.9 reshape.97
  366.7 3.2 reduce_sum.31
  (29 shorter events, 0.3 us)
Async XLA Ops:
  7.2 153.3 %copy-start = (bf16[1,384,4096]{2,1,0:T(8,128)(2,1)S(1)}, bf16[1,384,4096]{2,1,0:T(8,128)(2,1)}, u32[]{:S(2)}) copy-start(bf16[1,384,4096]{2,1,0:T(8,128)(2,1)} %param.11) | copy-start | bytes 9437188
  7.2 27.7 %all-gather.2.cloned.1.call-start = ((), (), s32[]{:S(2)}) async-start(), calls=%async_computation.6 | async-start | bytes 1310720 | tf_op jit(solution)/shard_map/all_gather | solution.py:54
  17.5 33.1 %all-to-all-start = ((bf16[8,64,1]{1,2,0:T(2,128)(2,1)}), bf16[8,64,1]{1,2,0:T(2,128)(2,1)S(1)}, u32[]{:S(2)}, u32[]{:S(2)}) async-start(bf16[8,64,1]{1,2,0:T(2,128)(2,1)} %all_to_all.50), calls=%async_computation | async-start | bytes 8192 | tf_op jit(solution)/shard_map/all_to_all | solution.py:72
  149.6 96.7 %all-to-all-start.1 = ((bf16[8,64,4096]{2,1,0:T(8,128)(2,1)}), bf16[8,64,4096]{2,1,0:T(8,128)(2,1)}, u32[]{:S(2)}, u32[]{:S(2)}) async-start(bf16[8,64,4096]{2,1,0:T(8,128)(2,1)} %get-tuple-element.23), calls=%async_computation.1 | async-start | bytes 8388608 | tf_op jit(solution)/shard_map/all_to_all | solution.py:71
  154.1 149.2 %reduce-scatter.2.cloned.1.call-start = ((), (), s32[]{:S(2)}) async-start(), calls=%async_computation.7 | async-start | bytes 5242880 | tf_op jit(solution)/shard_map/reduce_scatter | solution.py:94
  154.4 6.0 %copy-start.1 = (bf16[8,64,4096]{2,1,0:T(8,128)(2,1)S(1)}, bf16[8,64,4096]{2,1,0:T(8,128)(2,1)}, u32[]{:S(2)}) copy-start(bf16[8,64,4096]{2,1,0:T(8,128)(2,1)} %all_to_all.56) | copy-start | bytes 12582916
  252.7 2.4 copy-start.4
  252.7 2.4 copy-start.3
  266.0 40.1 %all-to-all-start.4 = ((f32[8,64,1]{1,2,0:T(1,128)}), f32[8,64,1]{1,2,0:T(1,128)S(1)}, u32[]{:S(2)}, u32[]{:S(2)}) async-start(f32[8,64,1]{1,2,0:T(1,128)} %bitcast.13), calls=%async_computation.5 | async-start | bytes 8192 | tf_op jit(solution)/shard_map/all_to_all | solution.py:99
  306.1 53.7 %all-to-all-start.3 = ((f32[8,64,1024]{2,1,0:T(8,128)}), f32[8,64,1024]{2,1,0:T(8,128)}, u32[]{:S(2)}, u32[]{:S(2)}) async-start(f32[8,64,1024]{2,1,0:T(8,128)} %convert.2), calls=%async_computation.4 | async-start | bytes 4194304 | tf_op jit(solution)/shard_map/all_to_all | solution.py:98
  311.6 5.9 %copy-start.2 = (bf16[8,64,4096]{2,1,0:T(8,128)(2,1)S(1)}, bf16[8,64,4096]{2,1,0:T(8,128)(2,1)}, u32[]{:S(2)}) copy-start(bf16[8,64,4096]{2,1,0:T(8,128)(2,1)} %all_to_all.56) | copy-start | bytes 12582916
  317.5 3.6 copy-start.5
Sparse Core Ops, SparseCore 0:
  9.5 19.4 all-gather.1
  259.8 43.4 reduce-scatter.1
where the time goes:
time: 378 us; the launch traced here: 377 us
  waiting for transfers between devices  145 us (38%)
  blocking collectives  105 us (28%)
  local copies, waits for them, and re-layouts  38.5 us (10%)
  matrix products  37.3 us (10%)
  starting transfers between devices  22.4 us (6%)
  between operations  14.2 us (4%)
  other arithmetic  13.9 us (4%)
    all_to_all x1, blocking collectives, per_device(): lax.all_to_all(send_rows, 'dp', split_axis=0, concat_axis=0, tiled=True)  99 us
    all_to_all x1, waiting for transfers between devices, per_device(): lax.all_to_all(send_up, 'dp', split_axis=0, concat_axis=0, tiled=True)  83.1 us
    reduce_scatter x1, waiting for transfers between devices, per_device(): lax.psum_scatter(part_all.astype(jnp.float32).astype(jnp.bfloat16), 'expe...  32.5 us
    all_to_all x1, waiting for transfers between devices, per_device(): lax.all_to_all(summed, 'dp', split_axis=0, concat_axis=0, tiled=True)  29 us
    dot_general x3, matrix products, contract_last(): lax.dot_general(left, right, (((1,), (1,)), ((), ())), preferred_element_...  15.1 us
    dot_general x3, matrix products, contract_first(): lax.dot_general(left, right, (((0,), (0,)), ((), ())), preferred_element_...  15.1 us
    gather x1, local copies, waits for them, and re-layouts, per_device(): tokens[token_of]  9.97 us
    gather x1, local copies, waits for them, and re-layouts, per_device(): full_up[token_of]  9.92 us
  transfers between devices with their start and end apart: 6, of which 3 were waited for; matrix products, arithmetic and copies ran while one was open for 17% of the time, Pallas kernels for 0%

commit v1 on v0

v1 whole, which is shorter than its diff:
```python
import jax
import jax.numpy as jnp
from jax import lax
from jax.sharding import PartitionSpec as P


def swish_pair(pre):
    sigma = jax.nn.sigmoid(pre)
    return (pre * sigma, sigma * (1.0 + pre * (1.0 - sigma)))


def contract_last(left, right):
    return lax.dot_general(
        left, right, (((1,), (1,)), ((), ())), preferred_element_type=jnp.float32
    )


def contract_first(left, right):
    return lax.dot_general(
        left, right, (((0,), (0,)), ((), ())), preferred_element_type=jnp.float32
    )


def expert_backward(inputs, upward, scale_col, w_g, w_u, w_d):
    pre_gate = contract_last(inputs, w_g)
    pre_up = contract_last(inputs, w_u)
    swish, slope = swish_pair(pre_gate)
    act = (swish * pre_up).astype(jnp.bfloat16)
    act_f = act.astype(jnp.float32)
    back = contract_last(upward, w_d)
    gate_term = jnp.sum(act_f * back, axis=1)
    scaled = (scale_col * act_f).astype(jnp.bfloat16)
    grad_down = contract_first(scaled, upward).astype(jnp.bfloat16)
    weighted = scale_col * back
    d_gate = (weighted * pre_up * slope).astype(jnp.bfloat16)
    d_up = (weighted * swish).astype(jnp.bfloat16)
    grad_gate = contract_first(d_gate, inputs).astype(jnp.bfloat16)
    grad_up = contract_first(d_up, inputs).astype(jnp.bfloat16)
    piece = jnp.dot(d_gate, w_g, preferred_element_type=jnp.float32)
    piece = piece + jnp.dot(d_up, w_u, preferred_element_type=jnp.float32)
    return (piece.astype(jnp.bfloat16), gate_term, grad_gate, grad_up, grad_down)


def per_device(tokens, upstream, gates, expert_ids, w_gate, w_up, w_down):
    groups = lax.axis_size("dp")
    experts = groups * w_gate.shape[0]
    tok_rows, width = tokens.shape
    top = expert_ids.shape[1]
    cap = 2 * tok_rows * top // experts
    part = upstream.shape[1]
    rows = experts * cap
    own = lax.axis_index("expert")
    tok_part = lax.dynamic_slice_in_dim(tokens, own * part, part, axis=1)
    flat = expert_ids.reshape(-1)
    count = flat.shape[0]
    earlier = jnp.arange(count)[None, :] < jnp.arange(count)[:, None]
    same = flat[:, None] == flat[None, :]
    position = jnp.sum((earlier & same).astype(jnp.int32), axis=1)
    slot = (flat * cap + position).reshape(tok_rows, top)
    hit = slot[None, :, :] == jnp.arange(rows, dtype=jnp.int32)[:, None, None]
    pick = jnp.sum(hit.astype(jnp.float32), axis=2).astype(jnp.bfloat16)
    scale = jnp.sum(jnp.where(hit, gates.astype(jnp.float32)[None], 0.0), axis=(1, 2))
    packed = jnp.concatenate([tok_part, upstream], axis=1)
    send = jnp.dot(pick, packed, preferred_element_type=jnp.float32).astype(jnp.bfloat16)
    send = jnp.concatenate(
        [send, jnp.broadcast_to(scale[:, None], (rows, 128)).astype(jnp.bfloat16)], axis=1
    )
    got = lax.all_to_all(send, "dp", split_axis=0, concat_axis=0, tiled=True)
    inputs = lax.all_gather(got[:, :part], "expert", axis=1, tiled=True)
    upward = lax.all_gather(got[:, part : 2 * part], "expert", axis=1, tiled=True)
    scale_col = got[:, 2 * part : 2 * part + 1].astype(jnp.float32)
    piece, term, grad_gate, grad_up, grad_down = expert_backward(
        inputs, upward, scale_col, w_gate[0], w_up[0], w_down[0]
    )
    total = lax.psum(term, "expert")
    summed = lax.psum_scatter(piece, "expert", scatter_dimension=1, tiled=True)
    high = total.astype(jnp.bfloat16)
    low = (total - high.astype(jnp.float32)).astype(jnp.bfloat16)
    lane = lax.broadcasted_iota(jnp.int32, (rows, 128), 1)
    tail = jnp.where(lane == 0, high[:, None], low[:, None])
    home = lax.all_to_all(
        jnp.concatenate([summed, tail], axis=1), "dp", split_axis=0, concat_axis=0, tiled=True
    )
    grad_x = contract_first(pick, home[:, :part]).astype(jnp.bfloat16)
    terms = home[:, part].astype(jnp.float32) + home[:, part + 1].astype(jnp.float32)
    grad_gates = jnp.sum(jnp.where(hit, terms[:, None, None], 0.0), axis=0)
    return (grad_x, grad_gates, grad_gate[None], grad_up[None], grad_down[None])


def solution(mesh):
    in_specs = (
        P("dp", None),
        P("dp", "expert"),
        P("dp", None),
        P("dp", None),
        P("dp", "expert", None),
        P("dp", "expert", None),
        P("dp", "expert", None),
    )
    out_specs = (
        P("dp", "expert"),
        P("dp", None),
        P("dp", "expert", None),
        P("dp", "expert", None),
        P("dp", "expert", None),
    )
    return jax.shard_map(
        per_device, mesh=mesh, in_specs=in_specs, out_specs=out_specs, check_vma=False
    )
```

time: 378 us -> 250 us (0.66)
  blocking collectives: 105 us -> 64.4 us
  local copies, waits for them, and re-layouts: 38.5 us -> 5.38 us
  waiting for transfers between devices: 145 us -> 115 us
  starting transfers between devices: 22.4 us -> 5.61 us
  other arithmetic: 13.9 us -> 7.47 us
    all_to_all x4 -> x1, waiting for transfers between devices: 112 us -> 15.6 us  [per_device(): lax.all_to_all(jnp.concatenate([summed, tail], axis=1), 'dp', split_axis=...]
    all_gather x1 -> x2, waiting for transfers between devices: 0.01 us -> 60.3 us  [the longest x1 31.5 us: per_device(): inputs = lax.all_gather(got[:, :part], 'expert', axis=1, tiled=True)]
    all_to_all x1, blocking collectives: 99 us -> 58.5 us  [per_device(): got = lax.all_to_all(send, 'dp', split_axis=0, concat_axis=0, tiled=True)]
    gather x5 -> x0, local copies, waits for them, and re-layouts: 29.3 us -> none  [the longest x1 9.97 us: per_device(): tokens[token_of]]
    all_to_all x4 -> x1, starting transfers between devices: 22.2 us -> 5.49 us  [per_device(): lax.all_to_all(jnp.concatenate([summed, tail], axis=1), 'dp', split_axis=...]
    reduce_scatter x1, waiting for transfers between devices: 32.5 us -> 38.5 us  [per_device(): summed = lax.psum_scatter(piece, 'expert', scatter_dimension=1, tiled=True)]
    select_n x3 -> x1, other arithmetic: 5.8 us -> 0.2 us  [per_device(): tail = jnp.where(lane == 0, high[:, None], low[:, None])]
    dot_general x3 -> x4, matrix products: 15.1 us -> 15.1 us  [contract_first(): lax.dot_general(left, right, (((0,), (0,)), ((), ())), preferred_element_...]
  transfers between devices with their start and end apart: 6 -> 4, of which waited for: 3 -> 4; matrix products, arithmetic and copies ran while one was open for 17% -> 9% of each run, Pallas kernels for 0% -> 0%
where the time goes in v1:
time: 250 us
  waiting for transfers between devices  115 us (46%)
  blocking collectives  64.4 us (26%)
  matrix products  37.9 us (15%)
  between operations  13.9 us (6%)
  other arithmetic  7.47 us (3%)
  starting transfers between devices  5.61 us (2%)
  local copies, waits for them, and re-layouts  5.38 us (2%)
    all_to_all x1, blocking collectives, per_device(): got = lax.all_to_all(send, 'dp', split_axis=0, concat_axis=0, tiled=True)  58.5 us
    reduce_scatter x1, waiting for transfers between devices, per_device(): summed = lax.psum_scatter(piece, 'expert', scatter_dimension=1, tiled=True)  38.5 us
    all_gather x1, waiting for transfers between devices, per_device(): inputs = lax.all_gather(got[:, :part], 'expert', axis=1, tiled=True)  31.5 us
    all_gather x1, waiting for transfers between devices, per_device(): upward = lax.all_gather(got[:, part:2 * part], 'expert', axis=1, tiled=True)  28.9 us
    all_to_all x1, waiting for transfers between devices, per_device(): lax.all_to_all(jnp.concatenate([summed, tail], axis=1), 'dp', split_axis=...  15.6 us
    dot_general x4, matrix products, contract_first(): lax.dot_general(left, right, (((0,), (0,)), ((), ())), preferred_element_...  15.1 us
    dot_general x3, matrix products, contract_last(): lax.dot_general(left, right, (((1,), (1,)), ((), ())), preferred_element_...  14.1 us
    psum x1, blocking collectives, per_device(): total = lax.psum(term, 'expert')  5.9 us
  transfers between devices with their start and end apart: 4, of which 4 were waited for; matrix products, arithmetic and copies ran while one was open for 9% of the time, Pallas kernels for 0%

profile of v1, /device:TPU:0, one launch (start us, length us, event | category | flops | bytes accessed | tf_op | source)
XLA Modules:
  0.0 249.7 jit_solution(17244349848035692851)
XLA Ops:
  7.2 0.0 copy-start
  7.2 0.0 all-gather.5.cloned.1.call-start
  7.2 0.9 copy.28
  8.2 0.1 eq.35
  8.3 0.2 convert_reduce_fusion.2
  8.5 0.1 reduce_sum.48
  8.6 0.1 copy.29
  8.7 0.7 multiply_add_fusion
  9.4 0.7 convert_element_type.79
  10.1 1.0 constant_dynamic-slice_fusion
  11.0 0.2 convert_reduce_fusion
  11.2 1.6 convolution_convert_fusion.3
  12.9 0.1 broadcast_in_dim.62
  13.0 0.2 pad_maximum_fusion
  13.2 58.5 %all_to_all.24 = bf16[8,64,2176]{2,1,0:T(8,128)(2,1)S(1)} all-to-all(bf16[8,64,2176]{2,1,0:T(8,128)(2,1)S(1)} %bitcast.39), channel_id=1, replica_groups=mesh['dp'=8,'expert'=4] {'dp'}, dimensions={0} | all-to-all | bytes 4456448 | tf_op jit(solution)/shard_map/all_to_all | solution.py:68
  71.7 1.4 copy-done.1
  73.0 1.6 fusion.25
  74.6 0.0 all-gather.5.cloned.1.call-update
  74.7 0.0 all-gather.3.cloned.1.call-start
  74.7 0.7 all-gather.3.cloned.1.call-update
  75.4 0.0 reduce-scatter.2.cloned.1.call-start
  75.5 1.0 convert_reduce_fusion.1
  76.5 31.5 %all-gather.5.cloned.1.call-done = bf16[512,4096]{1,0:T(8,128)(2,1)} async-done(((bf16[512,1024]{1,0:T(8,128)(2,1)}), bf16[512,4096]{1,0:T(8,128)(2,1)}) %all-gather.5.cloned.1.call-update) | async-done | bytes 4194320 | tf_op jit(solution)/shard_map/all_gather | solution.py:69
  108.0 0.0 copy-done
  108.0 5.0 %fusion.5 = f32[512,384]{0,1:T(8,128)} fusion(bf16[512,4096]{1,0:T(8,128)(2,1)} %all-gather.5.cloned.1.call-done, bf16[1,384,4096]{2,1,0:T(8,128)(2,1)S(1)} %copy-done), kind=kOutput, calls=%fused_computation.9 | convolution fusion | flops 1610612736 | bytes 8126464 | tf_op jit(solution)/shard_map/dot_general | solution.py:13
  113.0 0.0 copy-done.2
  113.0 0.0 copy-done.7
  113.0 2.7 %fusion.8 = f32[512,384]{0,1:T(8,128)} fusion(bf16[512,4096]{1,0:T(8,128)(2,1)S(1)} %copy-done.7, bf16[1,384,4096]{2,1,0:T(8,128)(2,1)S(1)} %copy-done.2), kind=kOutput, calls=%fused_computation.12 | convolution fusion | flops 1610612736 | bytes 8126464 | tf_op jit(solution)/shard_map/dot_general | solution.py:13
  115.7 28.9 %all-gather.3.cloned.1.call-done = bf16[512,4096]{1,0:T(8,128)(2,1)} async-done(((bf16[512,1024]{1,0:T(8,128)(2,1)}), bf16[512,4096]{1,0:T(8,128)(2,1)}) %all-gather.3.cloned.1.call-update) | async-done | bytes 4194320 | tf_op jit(solution)/shard_map/all_gather | solution.py:70
  144.6 6.4 %fusion.13 = (f32[512]{0:T(512)S(1)}, bf16[512,384]{0,1:T(8,128)(2,1)}, bf16[512,384]{0,1:T(8,128)(2,1)S(1)}, bf16[512,384]{0,1:T(8,128)(2,1)S(1)}) fusion(f32[512,384]{0,1:T(8,128)} %fusion.8, f32[512,384]{0,1:T(8,128)} %fusion.5, f32[512]{0:T(512)S(1)} %convert_reduce_fusion.1, bf16[512,4096]{1,0:T(8,128)(2,1)} %all-gather.3.cloned.1.call-done, ...), kind=kOutput, calls=%fused_computation.23 | convolution fusion | flops 1614347776 | bytes 10096640 | tf_op jit(solution)/shard_map/dot_general | solution.py:13
  151.0 2.4 fusion.3
  153.4 0.0 copy-done.6
  153.4 0.0 copy-done.4
  153.4 0.0 copy-done.3
  153.4 4.6 %add_convert_fusion = bf16[512,4096]{1,0:T(8,128)(2,1)} fusion(f32[512,4096]{1,0:T(8,128)S(1)} %fusion.3, bf16[512,384]{0,1:T(8,128)(2,1)S(1)} %get-tuple-element.14, bf16[1,384,4096]{2,1,0:T(8,128)(2,1)S(1)} %copy-done.3), kind=kOutput, calls=%fused_computation | convolution fusion | flops 1614807040 | bytes 16121856 | tf_op jit(solution)/shard_map/dot_general | solution.py:40
  158.0 0.0 reduce-scatter.2.cloned.1.call-update
  158.0 5.9 %psum.7 = f32[512]{0:T(512)S(1)} all-reduce(f32[512]{0:T(512)S(1)} %get-tuple-element.9), channel_id=1, replica_groups=mesh['dp'=8,'expert'=4] {'expert'}, use_global_device_ids=true, to_apply=%region_5.6 | all-reduce | flops 512 | bytes 4096 | tf_op jit(solution)/shard_map/psum | solution.py:75
  163.9 0.2 broadcast_select_fusion
  164.1 38.5 %reduce-scatter.2.cloned.1.call-done = bf16[512,1024]{1,0:T(8,128)(2,1)} async-done(((bf16[512,4096]{1,0:T(8,128)(2,1)}), bf16[512,1024]{1,0:T(8,128)(2,1)}) %reduce-scatter.2.cloned.1.call-update) | async-done | bytes 1048592 | tf_op jit(solution)/shard_map/reduce_scatter | solution.py:76
  202.6 2.4 pad_maximum_fusion.1
  205.0 5.5 %all-to-all-start.1 = ((bf16[8,64,1152]{2,1,0:T(8,128)(2,1)}), bf16[8,64,1152]{2,1,0:T(8,128)(2,1)}, u32[]{:S(2)}, u32[]{:S(2)}) async-start(bf16[8,64,1152]{2,1,0:T(8,128)(2,1)} %bitcast.40), calls=%async_computation.2 | async-start | bytes 2359296 | tf_op jit(solution)/shard_map/all_to_all | solution.py:81
  210.5 5.9 %fusion = bf16[1,384,4096]{2,1,0:T(8,128)(2,1)} fusion(bf16[512,384]{0,1:T(8,128)(2,1)} %copy-done.6, bf16[512,4096]{1,0:T(8,128)(2,1)} %all-gather.5.cloned.1.call-done), kind=kOutput, calls=%fused_computation.4 | convolution fusion | flops 1612185600 | bytes 7733248 | tf_op jit(solution)/shard_map/dot_general | solution.py:19
  216.5 3.5 %fusion.1 = bf16[1,384,4096]{2,1,0:T(8,128)(2,1)} fusion(bf16[512,384]{0,1:T(8,128)(2,1)S(1)} %copy-done.5, bf16[512,4096]{1,0:T(8,128)(2,1)S(1)} %copy-done.8), kind=kOutput, calls=%fused_computation.5 | convolution fusion | flops 1612185600 | bytes 7733248 | tf_op jit(solution)/shard_map/dot_general | solution.py:19
  219.9 3.5 %fusion.2 = bf16[1,384,4096]{2,1,0:T(8,128)(2,1)} fusion(bf16[512,4096]{1,0:T(8,128)(2,1)S(1)} %copy-done.9, bf16[512,384]{0,1:T(8,128)(2,1)S(1)} %copy-done.10, f32[512]{0:T(512)S(1)} %convert_reduce_fusion.1), kind=kOutput, calls=%fused_computation.6 | convolution fusion | flops 1612775424 | bytes 7735296 | tf_op jit(solution)/shard_map/dot_general | solution.py:19
  223.4 15.6 %all-to-all-done.1 = bf16[8,64,1152]{2,1,0:T(8,128)(2,1)} async-done(((bf16[8,64,1152]{2,1,0:T(8,128)(2,1)}), bf16[8,64,1152]{2,1,0:T(8,128)(2,1)}, u32[]{:S(2)}, u32[]{:S(2)}) %all-to-all-start.1) | async-done | bytes 1179680 | tf_op jit(solution)/shard_map/all_to_all | solution.py:81
  239.0 2.3 convolution_convert_fusion.4
  241.3 1.2 add_reduce_fusion
  242.5 0.7 select_reduce_fusion
  (16 shorter events, 0.0 us)
Async XLA Ops:
  7.2 100.8 %copy-start = (bf16[1,384,4096]{2,1,0:T(8,128)(2,1)S(1)}, bf16[1,384,4096]{2,1,0:T(8,128)(2,1)}, u32[]{:S(2)}) copy-start(bf16[1,384,4096]{2,1,0:T(8,128)(2,1)} %param.11) | copy-start | bytes 9437188
  7.2 100.8 %all-gather.5.cloned.1.call-start = ((), (), s32[]{:S(2)}) async-start(), calls=%async_computation.4 | async-start | bytes 5242880 | tf_op jit(solution)/shard_map/all_gather | solution.py:69
  71.7 1.4 copy-start.1
  74.7 69.9 %all-gather.3.cloned.1.call-start = ((), (), s32[]{:S(2)}) async-start(), calls=%async_computation.3 | async-start | bytes 5242880 | tf_op jit(solution)/shard_map/all_gather | solution.py:70
  75.4 127.2 %reduce-scatter.2.cloned.1.call-start = ((), (), s32[]{:S(2)}) async-start(), calls=%async_computation.5 | async-start | bytes 5242880 | tf_op jit(solution)/shard_map/reduce_scatter | solution.py:76
  108.0 5.0 %copy-start.2 = (bf16[1,384,4096]{2,1,0:T(8,128)(2,1)S(1)}, bf16[1,384,4096]{2,1,0:T(8,128)(2,1)}, u32[]{:S(2)}) copy-start(bf16[1,384,4096]{2,1,0:T(8,128)(2,1)} %param.12) | copy-start | bytes 9437188
  108.0 5.0 %copy-start.7 = (bf16[512,4096]{1,0:T(8,128)(2,1)S(1)}, bf16[512,4096]{1,0:T(8,128)(2,1)}, u32[]{:S(2)}) copy-start(bf16[512,4096]{1,0:T(8,128)(2,1)} %all-gather.5.cloned.1.call-done) | copy-start | bytes 12582916
  151.0 2.4 copy-start.6
  151.0 2.4 copy-start.4
  151.0 2.4 copy-start.3
  205.0 34.0 %all-to-all-start.1 = ((bf16[8,64,1152]{2,1,0:T(8,128)(2,1)}), bf16[8,64,1152]{2,1,0:T(8,128)(2,1)}, u32[]{:S(2)}, u32[]{:S(2)}) async-start(bf16[8,64,1152]{2,1,0:T(8,128)(2,1)} %bitcast.40), calls=%async_computation.2 | async-start | bytes 2359296 | tf_op jit(solution)/shard_map/all_to_all | solution.py:81
  210.5 5.9 %copy-start.5 = (bf16[512,384]{0,1:T(8,128)(2,1)S(1)}, bf16[512,384]{0,1:T(8,128)(2,1)}, u32[]{:S(2)}) copy-start(bf16[512,384]{0,1:T(8,128)(2,1)} %copy-done.4) | copy-start | bytes 1179652
  210.5 5.9 %copy-start.8 = (bf16[512,4096]{1,0:T(8,128)(2,1)S(1)}, bf16[512,4096]{1,0:T(8,128)(2,1)}, u32[]{:S(2)}) copy-start(bf16[512,4096]{1,0:T(8,128)(2,1)} %all-gather.5.cloned.1.call-done) | copy-start | bytes 12582916
  216.4 3.5 %copy-start.9 = (bf16[512,4096]{1,0:T(8,128)(2,1)S(1)}, bf16[512,4096]{1,0:T(8,128)(2,1)}, u32[]{:S(2)}) copy-start(bf16[512,4096]{1,0:T(8,128)(2,1)} %all-gather.3.cloned.1.call-done) | copy-start | bytes 12582916
  216.4 3.5 %copy-start.10 = (bf16[512,384]{0,1:T(8,128)(2,1)S(1)}, bf16[512,384]{0,1:T(8,128)(2,1)}, u32[]{:S(2)}) copy-start(bf16[512,384]{0,1:T(8,128)(2,1)} %get-tuple-element.10) | copy-start | bytes 1179652
Sparse Core Ops, SparseCore 0:
  74.8 33.1 all-gather.4
  110.1 34.4 all-gather.2
  158.1 44.4 reduce-scatter.1

commit v2 on v1

v2 whole, which is shorter than its diff:
```python
import functools

import jax
import jax.numpy as jnp
from jax import lax
from jax.experimental import pallas as pl
from jax.experimental.pallas import tpu as pltpu
from jax.sharding import PartitionSpec as P

MESH = pltpu.DeviceIdType.MESH if hasattr(pltpu, "DeviceIdType") else pl.DeviceIdType.MESH


def contract_last(left, right):
    return lax.dot_general(
        left, right, (((1,), (1,)), ((), ())), preferred_element_type=jnp.float32
    )


def contract_first(left, right):
    return lax.dot_general(
        left, right, (((0,), (0,)), ((), ())), preferred_element_type=jnp.float32
    )


def matmul(left, right):
    return jnp.dot(left, right, preferred_element_type=jnp.float32)


def kernel(
    groups, parts,
    send_t, send_u, send_s, w_g_hbm, w_u_hbm, w_d_hbm,
    home, home_s, out_g, out_u, out_d,
    recv_t, recv_u, recv_s, weights, pre, flipped, straight, grads,
    term, term_recv, total_term,
    pair_send, pair_recv, side_send, side_recv, own_sum, out_send,
    w_sem, g_sem, local_sem, recv_sem, scale_sem, dp_send, pair_fwd, side_fwd,
    scale_send, pair_send_sem, pair_recv_sem, side_send_sem, side_recv_sem,
    home_send, home_recv, term_send, term_sem, back_send, back_recv,
):
    me, own = lax.axis_index("dp"), lax.axis_index("expert")
    core, place = lax.rem(own, 2), lax.div(own, 2)
    places = parts // 2
    partner = place * 2 + (1 - core)
    cap, part = send_t.shape[1:]
    rows = groups * cap
    hid = weights.shape[2]
    sends, recvs = (send_t, send_u), (recv_t, recv_u)

    def ahead(k):
        return lax.rem(me + k, groups)

    def behind(k):
        return lax.rem(me + groups - k, groups)

    def aside(j):
        return lax.rem(place + j, places)

    def remote(src, dst, send_sem, sem, target):
        return pltpu.make_async_remote_copy(
            src_ref=src, dst_ref=dst, send_sem=send_sem, recv_sem=sem,
            device_id=target, device_id_type=MESH,
        )

    def arrived(ref, sem):
        pltpu.make_async_copy(ref, ref, sem).wait()

    loads = []
    for m, w_hbm in enumerate((w_g_hbm, w_u_hbm, w_d_hbm)):
        for j in range(parts):
            load = pltpu.make_async_copy(
                w_hbm.at[:, pl.ds(j * part, part)], weights.at[m, j], w_sem.at[m, j]
            )
            load.start()
            loads.append(load)

    barrier = pltpu.get_barrier_semaphore()
    for k in range(1, groups):
        pl.semaphore_signal(barrier, inc=1, device_id={"dp": ahead(k)}, device_id_type=MESH)
    for j in range(1, parts):
        pl.semaphore_signal(
            barrier, inc=1, device_id={"expert": lax.rem(own + j, parts)}, device_id_type=MESH
        )
    pl.semaphore_wait(barrier, groups + parts - 2)

    for k in range(1, groups):
        to = ahead(k)
        for t in range(2):
            if t == 0:
                remote(send_t.at[to], recv_t.at[own, me], dp_send.at[0],
                       recv_sem.at[0, own, me], {"dp": to}).start()
    for k in range(1, groups):
        to = ahead(k)
        remote(send_s.at[to], recv_s.at[me], scale_send, scale_sem.at[me], {"dp": to}).start()
        remote(send_u.at[to], recv_u.at[own, me], dp_send.at[1],
               recv_sem.at[1, own, me], {"dp": to}).start()
    keeps = []
    for t in range(2):
        keep = pltpu.make_async_copy(sends[t].at[me], recvs[t].at[own, me], local_sem.at[t])
        keep.start()
        keeps.append(keep)
    recv_s[me] = send_s[me]

    def relay(t, k):
        s = behind(k)
        spot = recvs[t].at[own, s]
        if k == 0:
            source = sends[t].at[me]
        else:
            arrived(spot, recv_sem.at[t, own, s])
            source = spot
        for j in range(1, places):
            remote(source, spot, side_fwd.at[t], recv_sem.at[t, own, s],
                   {"expert": aside(j) * 2 + core}).start()
        remote(source, spot, pair_fwd.at[t], recv_sem.at[t, own, s], {"expert": partner}).start()

    def pass_on(t, k):
        s = behind(k)
        for j in range(1, places):
            part_of = aside(j) * 2 + core
            spot = recvs[t].at[part_of, s]
            arrived(spot, recv_sem.at[t, part_of, s])
            remote(spot, spot, pair_fwd.at[t], recv_sem.at[t, part_of, s],
                   {"expert": partner}).start()

    def finish(t):
        keeps[t].wait()
        for k in range(groups):
            s = behind(k)
            for j in range(places):
                part_of = aside(j) * 2 + (1 - core)
                arrived(recvs[t].at[part_of, s], recv_sem.at[t, part_of, s])

    def forward_unit(m, j):
        loads[m * parts + j].wait()
        block = recvs[m // 2][j].reshape(rows, part)
        value = contract_last(weights[m, j], block)
        if j == 0:
            pre[m] = value
        else:
            pre[m] = pre[m] + value

    units = [(m, j) for m in range(2) for j in range(parts)]
    steps = [(t, k) for t in range(2) for k in range(groups)]
    lag = 2
    begin = groups + lag
    for i in range(len(steps) + lag):
        if i < len(steps):
            relay(*steps[i])
        if i >= lag:
            pass_on(*steps[i - lag])
        if i == begin - 1:
            finish(0)
        if i >= begin - 1:
            share = -(-len(units) // max(1, len(steps) + lag - i))
            for _ in range(share):
                if units:
                    forward_unit(*units.pop(0))
    for unit in units:
        forward_unit(*unit)
    finish(1)
    for j in range(parts):
        forward_unit(2, j)

    for k in range(1, groups):
        arrived(recv_s.at[behind(k)], scale_sem.at[behind(k)])
    scale = jnp.transpose(recv_s[...].reshape(rows, 128).astype(jnp.float32))[0:1, :]
    tile = 32
    term[...] = jnp.zeros_like(term)

    @pl.loop(0, hid // tile)
    def _(step):
        at = pl.ds(pl.multiple_of(step * tile, tile), tile)
        gate, up, back = pre[0, at, :], pre[1, at, :], pre[2, at, :]
        sigma = jax.nn.sigmoid(gate)
        swish = gate * sigma
        slope = sigma * (1.0 + gate * (1.0 - sigma))
        act = (swish * up).astype(jnp.bfloat16).astype(jnp.float32)
        term[...] += jnp.broadcast_to(jnp.sum(act * back, axis=0, keepdims=True), term.shape)
        weighted = scale * back
        flipped[0, at, :] = (weighted * up * slope).astype(jnp.bfloat16)
        flipped[1, at, :] = (weighted * swish).astype(jnp.bfloat16)
        flipped[2, at, :] = (scale * act).astype(jnp.bfloat16)

    for j in range(1, parts):
        remote(term, term_recv.at[own], term_send, term_sem.at[own],
               {"expert": lax.rem(own + j, parts)}).start()
    for m in range(2):
        straight[m] = jnp.transpose(flipped[m].astype(jnp.float32)).astype(jnp.bfloat16)

    block_rows = min(rows, 256)

    def piece(which, lo):
        at = pl.ds(lo, block_rows)
        value = matmul(straight[0, at, :], weights[0, which])
        return value + matmul(straight[1, at, :], weights[1, which])

    chunk = block_rows // cap
    for j in list(range(1, places)) + [0]:
        there = aside(j) * 2
        for lo in range(0, rows, block_rows):
            value = piece(there + 1 - core, lo).astype(jnp.bfloat16)
            pair_send[j, pl.ds(lo // cap, chunk)] = value.reshape(chunk, cap, part)
        pair = remote(pair_send.at[j], pair_recv.at[j], pair_send_sem.at[j],
                      pair_recv_sem.at[j], {"expert": partner})
        pair.start()
        for lo in range(0, rows, block_rows):
            value = piece(there + core, lo)
            own_sum[pl.ds(lo // cap, chunk)] = value.reshape(chunk, cap, part)
        pair.wait_recv()
        if j == 0:
            continue
        for k in list(range(1, groups)) + [0]:
            to = ahead(k)
            both = own_sum[to] + pair_recv[j, to].astype(jnp.float32)
            side_send[j, to] = both.astype(jnp.bfloat16)
            remote(side_send.at[j, to], side_recv.at[j, to], side_send_sem.at[j],
                   side_recv_sem.at[j, to], {"expert": there + core}).start()

    stores = []

    def grad_unit(m, j):
        block = recvs[m // 2][j].reshape(rows, part)
        grads[m, j] = matmul(flipped[m], block).astype(jnp.bfloat16)
        store = pltpu.make_async_copy(
            grads.at[m, j], (out_g, out_u, out_d)[m].at[:, pl.ds(j * part, part)], g_sem.at[m, j]
        )
        store.start()
        stores.append(store)

    for j in range(1, parts):
        arrived(term_recv.at[lax.rem(own + j, parts)], term_sem.at[lax.rem(own + j, parts)])
    term_recv[own] = term[...]
    total = term_recv[0]
    for j in range(1, parts):
        total = total + term_recv[j]
    total_term[...] = total
    home_s[me] = total
    for k in range(1, groups):
        remote(total_term, home_s.at[me], back_send, back_recv.at[me], {"dp": ahead(k)}).start()

    units = [(m, j) for m in range(3) for j in range(parts)]
    order = list(range(1, groups)) + [0]
    for i, k in enumerate(order):
        for _ in range(-(-len(units) // (len(order) - i))):
            grad_unit(*units.pop(0))
        to = ahead(k)
        value = own_sum[to] + pair_recv[0, to].astype(jnp.float32)
        for j in range(1, places):
            arrived(side_recv.at[j, to], side_recv_sem.at[j, to])
            value = value + side_recv[j, to].astype(jnp.float32)
        if k == 0:
            home[me] = value.astype(jnp.bfloat16)
        else:
            out_send[to] = value.astype(jnp.bfloat16)
            remote(out_send.at[to], home.at[me], home_send, home_recv.at[me], {"dp": to}).start()

    for k in range(1, groups):
        s = behind(k)
        arrived(home.at[s], home_recv.at[s])
        arrived(home_s.at[s], back_recv.at[s])
    for store in stores:
        store.wait()
    arrived(recv_s.at[pl.ds(0, groups - 1)], scale_send)
    arrived(home.at[pl.ds(0, groups - 1)], home_send)
    arrived(home_s.at[pl.ds(0, groups - 1)], back_send)
    arrived(term_recv.at[pl.ds(0, parts - 1)], term_send)
    for t in range(2):
        arrived(recvs[t].at[0, pl.ds(0, groups - 1)], dp_send.at[t])
        arrived(recvs[t].at[pl.ds(0, places)], pair_fwd.at[t])
        if places > 1:
            arrived(recvs[t].at[pl.ds(0, places - 1)], side_fwd.at[t])
    for j in range(places):
        arrived(pair_send.at[j], pair_send_sem.at[j])
        if j:
            arrived(side_send.at[j], side_send_sem.at[j])


def exchange(send_t, send_u, send_s, w_gate, w_up, w_down, parts):
    groups, cap, part = send_t.shape
    rows = groups * cap
    hid, width = w_gate.shape
    places = parts // 2
    bf, f32 = jnp.bfloat16, jnp.float32
    dma = pltpu.SemaphoreType.DMA
    vmem = pl.BlockSpec(memory_space=pltpu.VMEM)
    hbm = pl.BlockSpec(memory_space=pl.ANY)
    grad = jax.ShapeDtypeStruct((hid, width), bf)
    return pl.pallas_call(
        functools.partial(kernel, groups, parts),
        out_shape=(
            jax.ShapeDtypeStruct((groups, cap, part), bf),
            jax.ShapeDtypeStruct((groups, 8, rows), f32),
            grad, grad, grad,
        ),
        in_specs=[vmem] * 3 + [hbm] * 3,
        out_specs=(vmem, vmem, hbm, hbm, hbm),
        scratch_shapes=[
            pltpu.VMEM((parts, groups, cap, part), bf),
            pltpu.VMEM((parts, groups, cap, part), bf),
            pltpu.VMEM((groups, cap, 128), bf),
            pltpu.VMEM((3, parts, hid, part), bf),
            pltpu.VMEM((3, hid, rows), f32),
            pltpu.VMEM((3, hid, rows), bf),
            pltpu.VMEM((2, rows, hid), bf),
            pltpu.VMEM((3, parts, hid, part), bf),
            pltpu.VMEM((8, rows), f32),
            pltpu.VMEM((parts, 8, rows), f32),
            pltpu.VMEM((8, rows), f32),
            pltpu.VMEM((places, groups, cap, part), bf),
            pltpu.VMEM((places, groups, cap, part), bf),
            pltpu.VMEM((places, groups, cap, part), bf),
            pltpu.VMEM((places, groups, cap, part), bf),
            pltpu.VMEM((groups, cap, part), f32),
            pltpu.VMEM((groups, cap, part), bf),
            dma((3, parts)), dma((3, parts)), dma((2,)), dma((2, parts, groups)),
            dma((groups,)), dma((2,)), dma((2,)), dma((2,)), dma,
            dma((places,)), dma((places,)), dma((places,)), dma((places, groups)),
            dma, dma((groups,)), dma, dma((parts,)), dma, dma((groups,)),
        ],
        compiler_params=pltpu.CompilerParams(
            collective_id=0, has_side_effects=True, vmem_limit_bytes=62 * 1024 * 1024
        ),
    )(send_t, send_u, send_s, w_gate, w_up, w_down)


def per_device(tokens, upstream, gates, expert_ids, w_gate, w_up, w_down):
    groups = lax.axis_size("dp")
    parts = lax.axis_size("expert")
    experts = groups * w_gate.shape[0]
    tok_rows, width = tokens.shape
    top = expert_ids.shape[1]
    cap = 2 * tok_rows * top // experts
    part = upstream.shape[1]
    rows = experts * cap
    own = lax.axis_index("expert")
    tok_part = lax.dynamic_slice_in_dim(tokens, own * part, part, axis=1)
    flat = expert_ids.reshape(-1)
    count = flat.shape[0]
    earlier = jnp.arange(count)[None, :] < jnp.arange(count)[:, None]
    same = flat[:, None] == flat[None, :]
    position = jnp.sum((earlier & same).astype(jnp.int32), axis=1)
    slot = (flat * cap + position).reshape(tok_rows, top)
    hit = slot[None, :, :] == jnp.arange(rows, dtype=jnp.int32)[:, None, None]
    pick = jnp.sum(hit.astype(jnp.float32), axis=2).astype(jnp.bfloat16)
    scale = jnp.sum(jnp.where(hit, gates.astype(jnp.float32)[None], 0.0), axis=(1, 2))
    send_t = matmul(pick, tok_part).astype(jnp.bfloat16).reshape(groups, cap, part)
    send_u = matmul(pick, upstream).astype(jnp.bfloat16).reshape(groups, cap, part)
    send_s = jnp.broadcast_to(scale[:, None], (rows, 128)).astype(jnp.bfloat16)
    home, home_s, grad_gate, grad_up, grad_down = exchange(
        send_t, send_u, send_s.reshape(groups, cap, 128), w_gate[0], w_up[0], w_down[0], parts
    )
    grad_x = contract_first(pick, home.reshape(rows, part)).astype(jnp.bfloat16)
    terms = home_s[:, 0, :].reshape(groups, groups, cap)
    terms = lax.dynamic_index_in_dim(terms, lax.axis_index("dp"), 1, keepdims=False).reshape(rows)
    grad_gates = jnp.sum(jnp.where(hit, terms[:, None, None], 0.0), axis=0)
    return (grad_x, grad_gates, grad_gate[None], grad_up[None], grad_down[None])


def solution(mesh):
    in_specs = (
        P("dp", None),
        P("dp", "expert"),
        P("dp", None),
        P("dp", None),
        P("dp", "expert", None),
        P("dp", "expert", None),
        P("dp", "expert", None),
    )
    out_specs = (
        P("dp", "expert"),
        P("dp", None),
        P("dp", "expert", None),
        P("dp", "expert", None),
        P("dp", "expert", None),
    )
    return jax.shard_map(
        per_device, mesh=mesh, in_specs=in_specs, out_specs=out_specs, check_vma=False
    )
```

time: 250 us -> 132 us (0.53)
  waiting for transfers between devices: 115 us -> 0 us
  Pallas kernels: 0 us -> 108 us
  blocking collectives: 64.4 us -> 0 us
  matrix products: 37.9 us -> 6 us
  between operations: 13.9 us -> 0.68 us
  local copies, waits for them, and re-layouts: 5.38 us -> 11.9 us
  starting transfers between devices: 5.61 us -> 0 us
  other arithmetic: 7.47 us -> 2.52 us
    pallas_call x0 -> x1, Pallas kernels: none -> 108 us  [exchange(): pl.pallas_call(functools.partial(kernel, groups, parts), out_shape=(jax.S...]
    all_gather x2 -> x0, waiting for transfers between devices: 60.3 us -> none  [the longest x1 31.5 us: per_device(): inputs = lax.all_gather(got[:, :part], 'expert', axis=1, tiled=True)]
    all_to_all x1 -> x0, blocking collectives: 58.5 us -> none  [per_device(): got = lax.all_to_all(send, 'dp', split_axis=0, concat_axis=0, tiled=True)]
    reduce_scatter x1 -> x0, waiting for transfers between devices: 38.5 us -> none  [per_device(): summed = lax.psum_scatter(piece, 'expert', scatter_dimension=1, tiled=True)]
    dot_general x6 -> x2, matrix products: 22.7 us -> 3.73 us  [matmul(): return jnp.dot(left, right, preferred_element_type=jnp.float32)]
    all_to_all x1 -> x0, waiting for transfers between devices: 15.6 us -> none  [per_device(): lax.all_to_all(jnp.concatenate([summed, tail], axis=1), 'dp', split_axis=...]
    dot_general x4 -> x1, matrix products: 15.1 us -> 2.27 us  [contract_first(): lax.dot_general(left, right, (((0,), (0,)), ((), ())), preferred_element_...]
    unnamed x23 -> x10, local copies, waits for them, and re-layouts: 2.34 us -> 9.54 us
  transfers between devices with their start and end apart: 4 -> 0, of which waited for: 4 -> 0; matrix products, arithmetic and copies ran while one was open for 9% -> 0% of each run, Pallas kernels for 0% -> 0%
where the time goes in v2:
time: 132 us; the launch traced here: 129 us
  Pallas kernels  108 us (82%)
  local copies, waits for them, and re-layouts  11.9 us (9%)
  matrix products  6 us (5%)
  other arithmetic  2.52 us (2%)
    pallas_call x1, Pallas kernels, exchange(): pl.pallas_call(functools.partial(kernel, groups, parts), out_shape=(jax.S...  108 us
    unnamed x10, local copies, waits for them, and re-layouts  9.54 us
    dot_general x2, matrix products, matmul(): return jnp.dot(left, right, preferred_element_type=jnp.float32)  3.73 us

profile of v2, /device:TPU:0, one launch (start us, length us, event | category | flops | bytes accessed | tf_op | source)
XLA Modules:
  0.0 129.4 jit_solution(13895296323083529674)
XLA Ops:
  0.6 0.0 copy-start
  0.7 0.7 convert_element_type.34
  1.4 0.8 copy.22
  2.2 0.1 eq.28
  2.3 0.2 convert_reduce_fusion.1
  2.5 0.1 reduce_sum.39
  2.7 0.1 copy.23
  2.7 0.7 multiply_add_fusion
  3.4 0.2 select_reduce_fusion.1
  3.6 0.1 convert_element_type.36
  3.7 0.8 broadcast_in_dim.45.send_s
  4.5 0.0 copy-done
  4.5 1.4 %convolution_convert_fusion.1 = bf16[512,1024]{1,0:T(8,128)(2,1)} fusion(bf16[128,4096]{1,0:T(8,128)(2,1)S(1)} %copy-done, s32[]{:T(128)S(6)} %select_n.15, bf16[512,128]{1,0:T(8,128)(2,1)S(1)} %get-tuple-element.16), kind=kOutput, calls=%fused_computation.1 | convolution fusion | flops 134742016 | bytes 1441796 | tf_op jit(solution)/shard_map/dot_general | solution.py:26
  5.9 2.3 %convolution_convert_fusion = bf16[512,1024]{1,0:T(8,128)(2,1)} fusion(bf16[128,1024]{1,0:T(8,128)(2,1)} %param.8, bf16[512,128]{1,0:T(8,128)(2,1)S(1)} %get-tuple-element.16), kind=kOutput, calls=%fused_computation | convolution fusion | flops 134742016 | bytes 1441792 | tf_op jit(solution)/shard_map/dot_general | solution.py:26
  8.2 108.3 %shard_map.110 = (bf16[8,64,1024]{2,1,0:T(8,128)(2,1)}, f32[8,8,512]{2,1,0:T(8,128)}, bf16[384,4096]{1,0:T(8,128)(2,1)}, bf16[384,4096]{1,0:T(8,128)(2,1)}, bf16[384,4096]{1,0:T(8,128)(2,1)}) custom-call(bf16[8,64,1024]{2,1,0:T(8,128)(2,1)} %bitcast.14, bf16[8,64,1024]{2,1,0:T(8,128)(2,1)} %bitcast.15, bf16[8,64,128]{2,1,0:T(8,128)(2,1)} %broadcast_in_dim.45.send_s, ...), custom_call_target="tpu_custom_call" | custom-call | tf_op jit(solution)/shard_map/pallas_call | solution.py:288
  116.5 2.3 %convolution_convert_fusion.2 = bf16[128,1024]{1,0:T(8,128)(2,1)} fusion(bf16[512,1024]{1,0:T(8,128)(2,1)} %bitcast.22, bf16[512,128]{1,0:T(8,128)(2,1)S(1)} %get-tuple-element.16), kind=kOutput, calls=%fused_computation.2 | convolution fusion | flops 134348800 | bytes 1441792 | tf_op jit(solution)/shard_map/dot_general | solution.py:20
  118.8 0.9 slice_reduce_fusion
  119.8 0.1 reshape_squeeze.3
  119.9 0.1 broadcast_in_dim.46
  119.9 0.7 select_reduce_fusion
  120.7 0.0 copy-start.2
  120.7 4.1 %copy.27 = bf16[1,384,4096]{2,1,0:T(8,128)(2,1)} copy(bf16[1,384,4096]{2,1,0:T(8,128)(2,1)} %bitcast.18) | data formatting | bytes 6291456
  124.7 0.0 copy-done.2
  124.7 0.0 copy-start.1
  124.7 1.7 %copy.28 = bf16[1,384,4096]{2,1,0:T(8,128)(2,1)} copy(bf16[1,384,4096]{2,1,0:T(8,128)(2,1)S(1)} %bitcast.17) | data formatting | bytes 6291456
  126.4 1.4 %copy-done.1 = bf16[384,4096]{1,0:T(8,128)(2,1)S(1)} copy-done((bf16[384,4096]{1,0:T(8,128)(2,1)S(1)}, bf16[384,4096]{1,0:T(8,128)(2,1)}, u32[]{:S(2)}) %copy-start.1) | copy-done | bytes 3145752
  127.7 1.7 %copy.29 = bf16[1,384,4096]{2,1,0:T(8,128)(2,1)} copy(bf16[1,384,4096]{2,1,0:T(8,128)(2,1)S(1)} %bitcast.16) | data formatting | bytes 6291456
  (1 shorter events, 0.0 us)
Async XLA Ops:
  0.6 3.8 %copy-start = (bf16[128,4096]{1,0:T(8,128)(2,1)S(1)}, bf16[128,4096]{1,0:T(8,128)(2,1)}, u32[]{:S(2)}) copy-start(bf16[128,4096]{1,0:T(8,128)(2,1)} %param.7) | copy-start | bytes 3145732
  120.7 4.1 %copy-start.2 = (bf16[384,4096]{1,0:T(8,128)(2,1)S(1)}, bf16[384,4096]{1,0:T(8,128)(2,1)}, u32[]{:S(2)}) copy-start(bf16[384,4096]{1,0:T(8,128)(2,1)} %get-tuple-element.13) | copy-start | bytes 9437188
  124.7 3.0 %copy-start.1 = (bf16[384,4096]{1,0:T(8,128)(2,1)S(1)}, bf16[384,4096]{1,0:T(8,128)(2,1)}, u32[]{:S(2)}) copy-start(bf16[384,4096]{1,0:T(8,128)(2,1)} %get-tuple-element.14) | copy-start | bytes 9437188

commit v3 on v2

v3 whole, which is shorter than its diff:
```python
import functools

import jax
import jax.numpy as jnp
from jax import lax
from jax.experimental import pallas as pl
from jax.experimental.pallas import tpu as pltpu
from jax.sharding import PartitionSpec as P

MESH = pltpu.DeviceIdType.MESH if hasattr(pltpu, "DeviceIdType") else pl.DeviceIdType.MESH


def contract_last(left, right):
    return lax.dot_general(
        left, right, (((1,), (1,)), ((), ())), preferred_element_type=jnp.float32
    )


def contract_first(left, right):
    return lax.dot_general(
        left, right, (((0,), (0,)), ((), ())), preferred_element_type=jnp.float32
    )


def matmul(left, right):
    return jnp.dot(left, right, preferred_element_type=jnp.float32)


def kernel(
    groups, parts,
    send_t, send_u, send_s, w_g_hbm, w_u_hbm, w_d_hbm,
    home, home_s, out_g, out_u, out_d,
    recv_t, recv_u, recv_s, weights, pre, flipped, straight, grads,
    term, term_recv, total_term,
    pair_send, pair_recv, side_send, side_recv, own_sum, out_send,
    w_sem, g_sem, local_sem, recv_sem, scale_sem, dp_send, pair_fwd, side_fwd,
    scale_send, pair_send_sem, pair_recv_sem, side_send_sem, side_recv_sem,
    home_send, home_recv, term_send, term_sem, back_send, back_recv,
):
    me, own = lax.axis_index("dp"), lax.axis_index("expert")
    core, place = lax.rem(own, 2), lax.div(own, 2)
    places = parts // 2
    partner = place * 2 + (1 - core)
    cap, part = send_t.shape[1:]
    rows = groups * cap
    hid = weights.shape[2]
    sends, recvs = (send_t, send_u), (recv_t, recv_u)

    half = groups // 2
    span = half * cap
    odds = [k for k in range(groups // 2 - 1, 0, -1) if k % 2]
    shifts = [0, groups // 2] + odds
    shifts = shifts + [k for k in range(groups) if k not in shifts]

    def ahead(p):
        return lax.rem(me + shifts[p], groups)

    def behind(p):
        return lax.rem(me + groups - shifts[p], groups)

    def aside(j):
        return lax.rem(place + j, places)

    def remote(src, dst, send_sem, sem, target):
        return pltpu.make_async_remote_copy(
            src_ref=src, dst_ref=dst, send_sem=send_sem, recv_sem=sem,
            device_id=target, device_id_type=MESH,
        )

    def arrived(ref, sem):
        pltpu.make_async_copy(ref, ref, sem).wait()

    barrier = pltpu.get_barrier_semaphore()
    for p in range(1, groups):
        pl.semaphore_signal(barrier, inc=1, device_id={"dp": ahead(p)}, device_id_type=MESH)
    for j in range(1, parts):
        pl.semaphore_signal(
            barrier, inc=1, device_id={"expert": lax.rem(own + j, parts)}, device_id_type=MESH
        )
    keeps = []
    for t in range(2):
        keep = pltpu.make_async_copy(sends[t].at[me], recvs[t].at[own, 0], local_sem.at[t])
        keep.start()
        keeps.append(keep)
    loads = []
    for m, w_hbm in enumerate((w_g_hbm, w_u_hbm, w_d_hbm)):
        for j in range(parts):
            load = pltpu.make_async_copy(
                w_hbm.at[:, pl.ds(j * part, part)], weights.at[m, j], w_sem.at[m, j]
            )
            load.start()
            loads.append(load)
    pl.semaphore_wait(barrier, groups + parts - 2)

    def halves(h):
        return range(h * half, (h + 1) * half)

    for h in range(2):
        for t in range(2):
            for p in halves(h):
                if p == 0:
                    continue
                to = ahead(p)
                remote(sends[t].at[to], recvs[t].at[own, p], dp_send.at[t],
                       recv_sem.at[t, own, p], {"dp": to}).start()
                if t == 0:
                    remote(send_s.at[to], recv_s.at[p], scale_send, scale_sem.at[p],
                           {"dp": to}).start()
    recv_s[0] = send_s[me]

    def relay(t, p):
        spot = recvs[t].at[own, p]
        if p == 0:
            source = sends[t].at[me]
        else:
            arrived(spot, recv_sem.at[t, own, p])
            source = spot
        for j in range(1, places):
            remote(source, spot, side_fwd.at[t], recv_sem.at[t, own, p],
                   {"expert": aside(j) * 2 + core}).start()
        remote(source, spot, pair_fwd.at[t], recv_sem.at[t, own, p], {"expert": partner}).start()

    def pass_on(t, p):
        for j in range(1, places):
            part_of = aside(j) * 2 + core
            spot = recvs[t].at[part_of, p]
            arrived(spot, recv_sem.at[t, part_of, p])
            remote(spot, spot, pair_fwd.at[t], recv_sem.at[t, part_of, p],
                   {"expert": partner}).start()

    def finish(t, h):
        if h == 0:
            keeps[t].wait()
        for p in halves(h):
            for j in range(places):
                part_of = aside(j) * 2 + (1 - core)
                arrived(recvs[t].at[part_of, p], recv_sem.at[t, part_of, p])

    def rows_of(t, j, h):
        return recvs[t][j, h * half : (h + 1) * half].reshape(span, part)

    def forward_unit(m, j, h):
        if h == 0:
            loads[m * parts + j].wait()
        value = contract_last(weights[m, j], rows_of(m // 2, j, h))
        if j == 0:
            pre[h, m] = value
        else:
            pre[h, m] = pre[h, m] + value

    tile = 32

    def middle(h):
        for p in halves(h):
            if p:
                arrived(recv_s.at[p], scale_sem.at[p])
        scale = recv_s[h * half : (h + 1) * half].reshape(span, 128).astype(jnp.float32)
        scale = jnp.transpose(scale)[0:1, :]
        term[h] = jnp.zeros(term.shape[1:], term.dtype)

        @pl.loop(0, hid // tile)
        def _(step):
            at = pl.ds(pl.multiple_of(step * tile, tile), tile)
            gate, up, back = pre[h, 0, at, :], pre[h, 1, at, :], pre[h, 2, at, :]
            sigma = jax.nn.sigmoid(gate)
            swish = gate * sigma
            slope = sigma * (1.0 + gate * (1.0 - sigma))
            act = (swish * up).astype(jnp.bfloat16).astype(jnp.float32)
            line = jnp.sum(act * back, axis=0, keepdims=True)
            term[h] += jnp.broadcast_to(line, term.shape[1:])
            weighted = scale * back
            flipped[h, 0, at, :] = (weighted * up * slope).astype(jnp.bfloat16)
            flipped[h, 1, at, :] = (weighted * swish).astype(jnp.bfloat16)
            flipped[h, 2, at, :] = (scale * act).astype(jnp.bfloat16)

    def turn(m, h):
        straight[h, m] = jnp.transpose(flipped[h, m].astype(jnp.float32)).astype(jnp.bfloat16)

    def piece(which, h):
        value = matmul(straight[h, 0], weights[0, which])
        value = value + matmul(straight[h, 1], weights[1, which])
        return value.reshape(half, cap, part)

    def to_pair(j, h):
        at = pl.ds(h * half, half)
        pair_send[j, at] = piece(aside(j) * 2 + 1 - core, h).astype(jnp.bfloat16)
        remote(pair_send.at[j, at], pair_recv.at[j, at], pair_send_sem.at[j],
               pair_recv_sem.at[j, h], {"expert": partner}).start()

    def to_side(j, h):
        at = pl.ds(h * half, half)
        value = piece(aside(j) * 2 + core, h)
        arrived(pair_recv.at[j, at], pair_recv_sem.at[j, h])
        value = value + pair_recv[j, at].astype(jnp.float32)
        if j == 0:
            own_sum[at] = value
            return
        side_send[j, at] = value.astype(jnp.bfloat16)
        for p in list(halves(h))[::-1]:
            remote(side_send.at[j, p], side_recv.at[j, p], side_send_sem.at[j],
                   side_recv_sem.at[j, p], {"expert": aside(j) * 2 + core}).start()

    def go_home(p):
        value = own_sum[p]
        for j in range(1, places):
            arrived(side_recv.at[j, p], side_recv_sem.at[j, p])
            value = value + side_recv[j, p].astype(jnp.float32)
        if p == 0:
            home[me] = value.astype(jnp.bfloat16)
        else:
            out_send[p] = value.astype(jnp.bfloat16)
            remote(out_send.at[p], home.at[me], home_send, home_recv.at[p],
                   {"dp": behind(p)}).start()

    call = functools.partial

    def first_tasks(h):
        jobs = [call(finish, 0, h)]
        return jobs + [call(forward_unit, m, j, h) for m in range(2) for j in range(parts)]

    def second_tasks(h):
        jobs = [call(finish, 1, h)] + [call(forward_unit, 2, j, h) for j in range(parts)]
        jobs += [call(middle, h), call(turn, 0, h), call(turn, 1, h)]
        for j in list(range(1, places)) + [0]:
            jobs += [call(to_pair, j, h), call(to_side, j, h)]
        return jobs

    steps = [(t, p) for h in range(2) for t in range(2) for p in halves(h)]
    lag = 2
    queue = []
    for i in range(len(steps) + lag):
        if i < len(steps):
            relay(*steps[i])
        if i >= lag:
            pass_on(*steps[i - lag])
        if i == half - 1 + lag:
            queue += first_tasks(0)
        if i == 2 * half - 1 + lag:
            queue += second_tasks(0)
        if i == 3 * half - 1 + lag:
            queue += first_tasks(1)
        for _ in range(3):
            if queue:
                queue.pop(0)()
    for p in list(halves(0))[::-1]:
        queue.append(call(go_home, p))
    for job in queue:
        job()
    for job in second_tasks(1):
        job()

    for j in range(1, parts):
        remote(term, term_recv.at[own], term_send, term_sem.at[own],
               {"expert": lax.rem(own + j, parts)}).start()

    stores = []

    def grad_unit(m, j):
        value = matmul(flipped[0, m], rows_of(m // 2, j, 0))
        value = value + matmul(flipped[1, m], rows_of(m // 2, j, 1))
        grads[m, j] = value.astype(jnp.bfloat16)
        store = pltpu.make_async_copy(
            grads.at[m, j], (out_g, out_u, out_d)[m].at[:, pl.ds(j * part, part)], g_sem.at[m, j]
        )
        store.start()
        stores.append(store)

    units = [(m, j) for m in range(3) for j in range(parts)]
    for _ in range(2):
        grad_unit(*units.pop(0))
    for j in range(1, parts):
        arrived(term_recv.at[lax.rem(own + j, parts)], term_sem.at[lax.rem(own + j, parts)])
    term_recv[own] = term[...]
    total = term_recv[0]
    for j in range(1, parts):
        total = total + term_recv[j]
    total_term[...] = total
    home_s[me] = total
    for p in range(1, groups):
        remote(total_term, home_s.at[me], back_send, back_recv.at[p], {"dp": behind(p)}).start()

    order = list(halves(1))[::-1]
    for i, p in enumerate(order):
        for _ in range(-(-len(units) // (len(order) - i))):
            grad_unit(*units.pop(0))
        go_home(p)

    for p in range(1, groups):
        arrived(home.at[ahead(p)], home_recv.at[p])
        arrived(home_s.at[ahead(p)], back_recv.at[p])
    for store in stores:
        store.wait()
    arrived(recv_s.at[pl.ds(0, groups - 1)], scale_send)
    arrived(home.at[pl.ds(0, groups - 1)], home_send)
    arrived(home_s.at[pl.ds(0, groups - 1)], back_send)
    arrived(term_recv.at[pl.ds(0, parts - 1)], term_send)
    for t in range(2):
        arrived(recvs[t].at[0, pl.ds(0, groups - 1)], dp_send.at[t])
        arrived(recvs[t].at[pl.ds(0, places)], pair_fwd.at[t])
        if places > 1:
            arrived(recvs[t].at[pl.ds(0, places - 1)], side_fwd.at[t])
    for j in range(places):
        arrived(pair_send.at[j], pair_send_sem.at[j])
        if j:
            arrived(side_send.at[j], side_send_sem.at[j])


def exchange(send_t, send_u, send_s, w_gate, w_up, w_down, parts):
    groups, cap, part = send_t.shape
    rows = groups * cap
    hid, width = w_gate.shape
    places = parts // 2
    span = rows // 2
    bf, f32 = jnp.bfloat16, jnp.float32
    dma = pltpu.SemaphoreType.DMA
    vmem = pl.BlockSpec(memory_space=pltpu.VMEM)
    hbm = pl.BlockSpec(memory_space=pl.ANY)
    grad = jax.ShapeDtypeStruct((hid, width), bf)
    return pl.pallas_call(
        functools.partial(kernel, groups, parts),
        out_shape=(
            jax.ShapeDtypeStruct((groups, cap, part), bf),
            jax.ShapeDtypeStruct((groups, 2, 8, span), f32),
            grad, grad, grad,
        ),
        in_specs=[vmem] * 3 + [hbm] * 3,
        out_specs=(vmem, vmem, hbm, hbm, hbm),
        scratch_shapes=[
            pltpu.VMEM((parts, groups, cap, part), bf),
            pltpu.VMEM((parts, groups, cap, part), bf),
            pltpu.VMEM((groups, cap, 128), bf),
            pltpu.VMEM((3, parts, hid, part), bf),
            pltpu.VMEM((2, 3, hid, span), f32),
            pltpu.VMEM((2, 3, hid, span), bf),
            pltpu.VMEM((2, 2, span, hid), bf),
            pltpu.VMEM((3, parts, hid, part), bf),
            pltpu.VMEM((2, 8, span), f32),
            pltpu.VMEM((parts, 2, 8, span), f32),
            pltpu.VMEM((2, 8, span), f32),
            pltpu.VMEM((places, groups, cap, part), bf),
            pltpu.VMEM((places, groups, cap, part), bf),
            pltpu.VMEM((places, groups, cap, part), bf),
            pltpu.VMEM((places, groups, cap, part), bf),
            pltpu.VMEM((groups, cap, part), f32),
            pltpu.VMEM((groups, cap, part), bf),
            dma((3, parts)), dma((3, parts)), dma((2,)), dma((2, parts, groups)),
            dma((groups,)), dma((2,)), dma((2,)), dma((2,)), dma,
            dma((places,)), dma((places, 2)), dma((places,)), dma((places, groups)),
            dma, dma((groups,)), dma, dma((parts,)), dma, dma((groups,)),
        ],
        compiler_params=pltpu.CompilerParams(
            collective_id=0, has_side_effects=True, vmem_limit_bytes=62 * 1024 * 1024
        ),
    )(send_t, send_u, send_s, w_gate, w_up, w_down)


def per_device(tokens, upstream, gates, expert_ids, w_gate, w_up, w_down):
    groups = lax.axis_size("dp")
    parts = lax.axis_size("expert")
    experts = groups * w_gate.shape[0]
    tok_rows, width = tokens.shape
    top = expert_ids.shape[1]
    cap = 2 * tok_rows * top // experts
    part = upstream.shape[1]
    rows = experts * cap
    own = lax.axis_index("expert")
    tok_part = lax.dynamic_slice_in_dim(tokens, own * part, part, axis=1)
    flat = expert_ids.reshape(-1)
    count = flat.shape[0]
    earlier = jnp.arange(count)[None, :] < jnp.arange(count)[:, None]
    same = flat[:, None] == flat[None, :]
    position = jnp.sum((earlier & same).astype(jnp.int32), axis=1)
    slot = (flat * cap + position).reshape(tok_rows, top)
    hit = slot[None, :, :] == jnp.arange(rows, dtype=jnp.int32)[:, None, None]
    pick = jnp.sum(hit.astype(jnp.float32), axis=2).astype(jnp.bfloat16)
    scale = jnp.sum(jnp.where(hit, gates.astype(jnp.float32)[None], 0.0), axis=(1, 2))
    send_t = matmul(pick, tok_part).astype(jnp.bfloat16).reshape(groups, cap, part)
    send_u = matmul(pick, upstream).astype(jnp.bfloat16).reshape(groups, cap, part)
    send_s = jnp.broadcast_to(scale[:, None], (rows, 128)).astype(jnp.bfloat16)
    home, home_s, grad_gate, grad_up, grad_down = exchange(
        send_t, send_u, send_s.reshape(groups, cap, 128), w_gate[0], w_up[0], w_down[0], parts
    )
    grad_x = contract_first(pick, home.reshape(rows, part)).astype(jnp.bfloat16)
    half = groups // 2
    odds = [k for k in range(half - 1, 0, -1) if k % 2]
    shifts = [0, half] + odds
    shifts = jnp.array(shifts + [k for k in range(groups) if k not in shifts])
    away = lax.rem(jnp.arange(groups) - lax.axis_index("dp") + groups, groups)
    terms = home_s[:, :, 0, :].reshape(groups, groups, cap)
    mine = (shifts[None, :] == away[:, None])[:, :, None]
    terms = jnp.sum(jnp.where(mine, terms, 0.0), axis=1).reshape(rows)
    grad_gates = jnp.sum(jnp.where(hit, terms[:, None, None], 0.0), axis=0)
    return (grad_x, grad_gates, grad_gate[None], grad_up[None], grad_down[None])


def solution(mesh):
    in_specs = (
        P("dp", None),
        P("dp", "expert"),
        P("dp", None),
        P("dp", None),
        P("dp", "expert", None),
        P("dp", "expert", None),
        P("dp", "expert", None),
    )
    out_specs = (
        P("dp", "expert"),
        P("dp", None),
        P("dp", "expert", None),
        P("dp", "expert", None),
        P("dp", "expert", None),
    )
    return jax.shard_map(
        per_device, mesh=mesh, in_specs=in_specs, out_specs=out_specs, check_vma=False
    )
```

time: 132 us -> 149 us (1.13); the launches traced: 129 us -> 148 us
  Pallas kernels: 108 us -> 127 us
    pallas_call x1, Pallas kernels: 108 us -> 127 us  [exchange(): pl.pallas_call(functools.partial(kernel, groups, parts), out_shape=(jax.S...]
    unnamed x10 -> x12, local copies, waits for them, and re-layouts: 9.54 us -> 9.63 us
where the time goes in v3:
time: 149 us; the launch traced here: 148 us
  Pallas kernels  127 us (85%)
  local copies, waits for them, and re-layouts  12 us (8%)
  matrix products  6.01 us (4%)
  other arithmetic  2.61 us (2%)
    pallas_call x1, Pallas kernels, exchange(): pl.pallas_call(functools.partial(kernel, groups, parts), out_shape=(jax.S...  127 us
    unnamed x12, local copies, waits for them, and re-layouts  9.63 us
    dot_general x2, matrix products, matmul(): return jnp.dot(left, right, preferred_element_type=jnp.float32)  3.74 us

profile of v3, /device:TPU:0, one launch (start us, length us, event | category | flops | bytes accessed | tf_op | source)
XLA Modules:
  0.0 148.2 jit_solution(7393347972741246754)
XLA Ops:
  0.6 0.0 copy-start
  0.7 0.9 copy.23
  1.5 0.1 eq.45
  1.7 0.2 convert_reduce_fusion.1
  1.9 0.1 reduce_sum.48
  2.0 0.1 copy.24
  2.1 0.7 multiply_add_fusion
  2.8 0.7 convert_element_type.34
  3.4 0.2 select_reduce_fusion.1
  3.6 0.0 copy-done
  3.6 1.4 convolution_convert_fusion.1
  5.0 2.3 %convolution_convert_fusion = bf16[512,1024]{1,0:T(8,128)(2,1)} fusion(bf16[128,1024]{1,0:T(8,128)(2,1)} %param.9, bf16[512,128]{1,0:T(8,128)(2,1)S(1)} %get-tuple-element.16), kind=kOutput, calls=%fused_computation | convolution fusion | flops 134742016 | bytes 1441792 | tf_op jit(solution)/shard_map/dot_general | solution.py:26
  7.3 0.1 convert_element_type.36
  7.4 0.8 broadcast_in_dim.60.send_s
  8.2 0.0 copy-start.3
  8.2 127.0 %shard_map.119 = (bf16[8,64,1024]{2,1,0:T(8,128)(2,1)}, f32[8,2,8,256]{3,2,1,0:T(8,128)}, bf16[384,4096]{1,0:T(8,128)(2,1)}, bf16[384,4096]{1,0:T(8,128)(2,1)}, bf16[384,4096]{1,0:T(8,128)(2,1)}) custom-call(bf16[8,64,1024]{2,1,0:T(8,128)(2,1)} %bitcast.14, bf16[8,64,1024]{2,1,0:T(8,128)(2,1)} %bitcast.15, bf16[8,64,128]{2,1,0:T(8,128)(2,1)} %broadcast_in_dim.60.send_s, ...), custom_call_target="tpu_custom_call" | custom-call | tf_op jit(solution)/shard_map/pallas_call | solution.py:319
  135.2 2.3 %convolution_convert_fusion.2 = bf16[128,1024]{1,0:T(8,128)(2,1)} fusion(bf16[512,1024]{1,0:T(8,128)(2,1)} %bitcast.22, bf16[512,128]{1,0:T(8,128)(2,1)S(1)} %get-tuple-element.16), kind=kOutput, calls=%fused_computation.2 | convolution fusion | flops 134348800 | bytes 1441792 | tf_op jit(solution)/shard_map/dot_general | solution.py:20
  137.5 1.0 slice_reduce_fusion
  138.4 0.1 reshape_squeeze.3
  138.5 0.0 copy-done.3
  138.5 0.1 broadcast_compare_fusion
  138.6 0.1 select_reduce_fusion.2
  138.7 0.1 broadcast_in_dim.63
  138.8 0.7 select_reduce_fusion
  139.5 0.0 copy-start.2
  139.5 4.1 %copy.28 = bf16[1,384,4096]{2,1,0:T(8,128)(2,1)} copy(bf16[1,384,4096]{2,1,0:T(8,128)(2,1)} %bitcast.18) | data formatting | bytes 6291456
  143.6 0.0 copy-done.2
  143.6 0.0 copy-start.1
  143.6 1.7 %copy.29 = bf16[1,384,4096]{2,1,0:T(8,128)(2,1)} copy(bf16[1,384,4096]{2,1,0:T(8,128)(2,1)S(1)} %bitcast.17) | data formatting | bytes 6291456
  145.2 1.4 copy-done.1
  146.6 1.7 %copy.30 = bf16[1,384,4096]{2,1,0:T(8,128)(2,1)} copy(bf16[1,384,4096]{2,1,0:T(8,128)(2,1)S(1)} %bitcast.16) | data formatting | bytes 6291456
  (1 shorter events, 0.0 us)
Async XLA Ops:
  0.6 3.0 %copy-start = (bf16[128,4096]{1,0:T(8,128)(2,1)S(1)}, bf16[128,4096]{1,0:T(8,128)(2,1)}, u32[]{:S(2)}) copy-start(bf16[128,4096]{1,0:T(8,128)(2,1)} %param.8) | copy-start | bytes 3145732
  8.2 130.3 %copy-start.3 = (s32[8]{0:T(128)S(1)}, s32[8]{0:T(128)}, u32[]{:S(2)}) copy-start(s32[8]{0:T(128)} %constant.26.clone) | copy-start | bytes 100
  139.5 4.1 %copy-start.2 = (bf16[384,4096]{1,0:T(8,128)(2,1)S(1)}, bf16[384,4096]{1,0:T(8,128)(2,1)}, u32[]{:S(2)}) copy-start(bf16[384,4096]{1,0:T(8,128)(2,1)} %get-tuple-element.13) | copy-start | bytes 9437188
  143.6 3.0 %copy-start.1 = (bf16[384,4096]{1,0:T(8,128)(2,1)S(1)}, bf16[384,4096]{1,0:T(8,128)(2,1)}, u32[]{:S(2)}) copy-start(bf16[384,4096]{1,0:T(8,128)(2,1)} %get-tuple-element.14) | copy-start | bytes 9437188

commit v4 on v2

--- a/solution.py
+++ b/solution.py
@@ -46,11 +46,19 @@
     hid = weights.shape[2]
     sends, recvs = (send_t, send_u), (recv_t, recv_u)
 
+    paired = groups & (groups - 1) == 0
+
+    def crossed(k):
+        spot = me
+        for bit in [1 << b for b in range(groups.bit_length()) if k >> b & 1]:
+            spot = spot + bit * (1 - 2 * lax.rem(lax.div(me, bit), 2))
+        return spot
+
     def ahead(k):
-        return lax.rem(me + k, groups)
+        return crossed(k) if paired else lax.rem(me + k, groups)
 
     def behind(k):
-        return lax.rem(me + groups - k, groups)
+        return crossed(k) if paired else lax.rem(me + groups - k, groups)
 
     def aside(j):
         return lax.rem(place + j, places)

time: 132 us -> 127 us (0.962)
  Pallas kernels: 108 us -> 104 us
    pallas_call x1, Pallas kernels: 108 us -> 104 us  [exchange(): pl.pallas_call(functools.partial(kernel, groups, parts), out_shape=(jax.S...]
where the time goes in v4:
time: 127 us; the launch traced here: 125 us
  Pallas kernels  104 us (82%)
  local copies, waits for them, and re-layouts  11.9 us (9%)
  matrix products  6 us (5%)
  other arithmetic  2.52 us (2%)
    pallas_call x1, Pallas kernels, exchange(): pl.pallas_call(functools.partial(kernel, groups, parts), out_shape=(jax.S...  104 us
    unnamed x10, local copies, waits for them, and re-layouts  9.54 us
    dot_general x2, matrix products, matmul(): return jnp.dot(left, right, preferred_element_type=jnp.float32)  3.73 us

profile of v4, /device:TPU:0, one launch (start us, length us, event | category | flops | bytes accessed | tf_op | source)
XLA Modules:
  0.0 125.4 jit_solution(10192943422890829041)
XLA Ops:
  0.6 0.0 copy-start
  0.7 0.7 convert_element_type.34
  1.4 0.8 copy.22
  2.2 0.1 eq.28
  2.3 0.2 convert_reduce_fusion.1
  2.5 0.1 reduce_sum.39
  2.7 0.1 copy.23
  2.7 0.7 multiply_add_fusion
  3.4 0.2 select_reduce_fusion.1
  3.6 0.1 convert_element_type.36
  3.7 0.8 broadcast_in_dim.45.send_s
  4.5 0.0 copy-done
  4.5 1.4 %convolution_convert_fusion.1 = bf16[512,1024]{1,0:T(8,128)(2,1)} fusion(bf16[128,4096]{1,0:T(8,128)(2,1)S(1)} %copy-done, s32[]{:T(128)S(6)} %select_n.15, bf16[512,128]{1,0:T(8,128)(2,1)S(1)} %get-tuple-element.16), kind=kOutput, calls=%fused_computation.1 | convolution fusion | flops 134742016 | bytes 1441796 | tf_op jit(solution)/shard_map/dot_general | solution.py:26
  5.9 2.3 %convolution_convert_fusion = bf16[512,1024]{1,0:T(8,128)(2,1)} fusion(bf16[128,1024]{1,0:T(8,128)(2,1)} %param.8, bf16[512,128]{1,0:T(8,128)(2,1)S(1)} %get-tuple-element.16), kind=kOutput, calls=%fused_computation | convolution fusion | flops 134742016 | bytes 1441792 | tf_op jit(solution)/shard_map/dot_general | solution.py:26
  8.2 104.3 %shard_map.110 = (bf16[8,64,1024]{2,1,0:T(8,128)(2,1)}, f32[8,8,512]{2,1,0:T(8,128)}, bf16[384,4096]{1,0:T(8,128)(2,1)}, bf16[384,4096]{1,0:T(8,128)(2,1)}, bf16[384,4096]{1,0:T(8,128)(2,1)}) custom-call(bf16[8,64,1024]{2,1,0:T(8,128)(2,1)} %bitcast.14, bf16[8,64,1024]{2,1,0:T(8,128)(2,1)} %bitcast.15, bf16[8,64,128]{2,1,0:T(8,128)(2,1)} %broadcast_in_dim.45.send_s, ...), custom_call_target="tpu_custom_call" | custom-call | tf_op jit(solution)/shard_map/pallas_call | solution.py:296
  112.5 2.3 %convolution_convert_fusion.2 = bf16[128,1024]{1,0:T(8,128)(2,1)} fusion(bf16[512,1024]{1,0:T(8,128)(2,1)} %bitcast.22, bf16[512,128]{1,0:T(8,128)(2,1)S(1)} %get-tuple-element.16), kind=kOutput, calls=%fused_computation.2 | convolution fusion | flops 134348800 | bytes 1441792 | tf_op jit(solution)/shard_map/dot_general | solution.py:20
  114.8 0.9 slice_reduce_fusion
  115.7 0.1 reshape_squeeze.3
  115.8 0.1 broadcast_in_dim.46
  115.9 0.7 select_reduce_fusion
  116.6 0.0 copy-start.2
  116.6 4.1 %copy.27 = bf16[1,384,4096]{2,1,0:T(8,128)(2,1)} copy(bf16[1,384,4096]{2,1,0:T(8,128)(2,1)} %bitcast.18) | data formatting | bytes 6291456
  120.7 0.0 copy-done.2
  120.7 0.0 copy-start.1
  120.7 1.7 %copy.28 = bf16[1,384,4096]{2,1,0:T(8,128)(2,1)} copy(bf16[1,384,4096]{2,1,0:T(8,128)(2,1)S(1)} %bitcast.17) | data formatting | bytes 6291456
  122.3 1.4 %copy-done.1 = bf16[384,4096]{1,0:T(8,128)(2,1)S(1)} copy-done((bf16[384,4096]{1,0:T(8,128)(2,1)S(1)}, bf16[384,4096]{1,0:T(8,128)(2,1)}, u32[]{:S(2)}) %copy-start.1) | copy-done | bytes 3145752
  123.7 1.7 %copy.29 = bf16[1,384,4096]{2,1,0:T(8,128)(2,1)} copy(bf16[1,384,4096]{2,1,0:T(8,128)(2,1)S(1)} %bitcast.16) | data formatting | bytes 6291456
  (1 shorter events, 0.0 us)
Async XLA Ops:
  0.6 3.8 %copy-start = (bf16[128,4096]{1,0:T(8,128)(2,1)S(1)}, bf16[128,4096]{1,0:T(8,128)(2,1)}, u32[]{:S(2)}) copy-start(bf16[128,4096]{1,0:T(8,128)(2,1)} %param.7) | copy-start | bytes 3145732
  116.6 4.1 %copy-start.2 = (bf16[384,4096]{1,0:T(8,128)(2,1)S(1)}, bf16[384,4096]{1,0:T(8,128)(2,1)}, u32[]{:S(2)}) copy-start(bf16[384,4096]{1,0:T(8,128)(2,1)} %get-tuple-element.13) | copy-start | bytes 9437188
  120.7 3.0 %copy-start.1 = (bf16[384,4096]{1,0:T(8,128)(2,1)S(1)}, bf16[384,4096]{1,0:T(8,128)(2,1)}, u32[]{:S(2)}) copy-start(bf16[384,4096]{1,0:T(8,128)(2,1)} %get-tuple-element.14) | copy-start | bytes 9437188
